TPU v7x, 128 devices: a whole 4x4x4 slice. The times are simulated.
128 devices in a mesh: smp: 32 (over x, z, y_lo), col: 2 (over core), slab: 2 (over y_hi).
Axes of the slice: x: 4, y: 4 (y_hi: 2, y_lo: 2; y = y_hi * 2 + y_lo), z: 4, core: 2. Of those that a mesh axis runs over, the one named last changes fastest.
Arguments:
- jacobian: bfloat16 [1024, 32, 16384], P('smp', 'slab', 'col'), may hold values from -0.005722046 to 0.005722046
- local_energy: float32 [1024], P('smp'), may hold values from -6 to 6
Outputs:
- update: float32 [32, 16384], P('slab', ('col', 'smp'))
All inputs are finite; a program needn't handle non-finite values.
Results may differ from a plain program's by a relative error of at most 0.0085.
Values may be sent and summed in bfloat16 or wider, within the bound.
A program may use at most 192 MiB of HBM per device.

v0:
```python
import jax
import jax.numpy as jnp
from jax import lax
from jax.sharding import PartitionSpec as P

SLABS = 32
SLAB_COLS = 16384


def shards(jacobian, local_energy):
    energies = lax.all_gather(local_energy, "smp", axis=0, tiled=True)
    samples = energies.shape[0]
    root_count = jnp.sqrt(jnp.float32(samples))
    eps = (energies - jnp.mean(energies)) / root_count
    columns = lax.all_to_all(jacobian, "smp", split_axis=2, concat_axis=0, tiled=True)
    slab_count = columns.shape[1]
    width = columns.shape[2]
    values = columns.astype(jnp.float32)
    mean_row = jnp.mean(values, axis=0, keepdims=True)
    centered = (
        ((values - mean_row) / root_count).astype(jnp.bfloat16).reshape(samples, slab_count * width)
    )
    partial_gram = jnp.dot(centered, centered.T, preferred_element_type=jnp.float32)
    gram = lax.psum(partial_gram, ("smp", "col", "slab"))
    shift = 0.01 * jnp.trace(gram) / samples
    factor = jnp.linalg.cholesky(gram + shift * jnp.eye(samples, dtype=jnp.float32))
    middle = lax.linalg.triangular_solve(factor, eps[:, None], left_side=True, lower=True)
    coeffs = lax.linalg.triangular_solve(
        factor, middle, left_side=True, lower=True, transpose_a=True
    )[:, 0]
    delta = jnp.dot(coeffs, centered.astype(jnp.float32), precision=lax.Precision.HIGHEST)
    squared = lax.psum(jnp.sum(delta * delta), ("smp", "col", "slab"))
    limit = 0.3 * jnp.sqrt(jnp.float32(SLABS * SLAB_COLS))
    scaled = -jnp.minimum(1.0, limit / jnp.sqrt(squared)) * delta
    return scaled.reshape(slab_count, width)


def solution(mesh):
    in_specs = (P("smp", "slab", "col"), P("smp"))
    out_specs = P("slab", ("col", "smp"))
    return jax.shard_map(shards, mesh=mesh, in_specs=in_specs, out_specs=out_specs, check_vma=False)
```

profile of v0, /device:TPU:1, one launch (start us, length us, event | category | flops | bytes accessed | tf_op | source)
XLA Modules:
  0.0 897.0 jit_solution(18186082243385075913)
XLA Ops:
  6.5 45.6 %copy.65 = bf16[32,16,8192]{0,1,2:T(8,128)(2,1)} copy(bf16[32,16,8192]{2,1,0:T(8,128)(2,1)} %param.2) | data formatting | bytes 16777216 | tf_op args[0]
  52.1 39.8 %reshape.341 = bf16[32,2,65536]{2,1,0:T(2,128)(2,1)} reshape(bf16[8192,16,32]{2,1,0:T(8,128)(2,1)} %bitcast.340) | data formatting | bytes 16777216
  91.9 105.1 %all_to_all.4 = bf16[32,2,65536]{2,1,0:T(2,128)(2,1)} all-to-all(bf16[32,2,65536]{2,1,0:T(2,128)(2,1)} %reshape.341), channel_id=1, replica_groups=mesh['smp'=32,'col'=2,'slab'=2] {'smp'}, dimensions={0} | all-to-all | bytes 16777216 | tf_op jit(solution)/shard_map/all_to_all | solution.py:15
  197.0 30.6 %reshape.342 = bf16[8192,16,32]{2,1,0:T(8,128)(2,1)} reshape(bf16[32,2,65536]{2,1,0:T(2,128)(2,1)} %all_to_all.4) | data formatting | bytes 16777216
  227.6 44.0 %copy.66 = f32[32,16,32,256]{3,1,0,2:T(8,128)} copy(bf16[32,16,32,256]{0,1,3,2:T(8,128)(2,1)} %bitcast.339) | data formatting | bytes 25165824 | tf_op jit(solution)/shard_map/convert_element_type | solution.py:18
  271.6 6.9 bitcast_reduce_fusion
  278.5 7.2 fusion.1
  288.9 16.6 %fusion.5 = f32[1024,1024]{0,1:T(8,128)} fusion(bf16[1024,16,256]{2,1,0:T(8,128)(2,1)S(1)} %bitcast.342), kind=kOutput, calls=%fused_computation.15 | convolution fusion | flops 8589934592 | bytes 12582912 | tf_op jit(solution)/shard_map/dot_general | solution.py:23
  307.8 65.8 %all-reduce.1 = f32[1024]{0:T(1024)S(1)} all-reduce(f32[1024]{0:T(1024)S(1)} %dynamic-update-slice.47), channel_id=1, replica_groups=mesh['smp'=32,'col'=2,'slab'=2] {'smp'}, use_global_device_ids=true, to_apply=%add.1 | all-reduce | flops 1024 | bytes 8192
  375.0 12.3 %copy.96 = bf16[128,8,16,256]{3,1,2,0:T(8,128)(2,1)} copy(bf16[128,8,16,256]{3,2,1,0:T(8,128)(2,1)} %bitcast.343) | data formatting | bytes 16777216
  387.3 73.0 %all-reduce.4.cloned.1.call-done = f32[1024,1024]{0,1:T(8,128)} async-done(((f32[1024,1024]{0,1:T(8,128)}), f32[1024,1024]{0,1:T(8,128)}) %all-reduce.4.cloned.1.call-update) | async-done | bytes 4194320 | tf_op jit(solution)/shard_map/psum | solution.py:24
  468.6 5.5 copy.70
  480.6 11.7 %cholesky.222 = f32[128,128]{1,0:T(8,128)S(1)} custom-call(f32[128,128]{1,0:T(8,128)S(1)} %cholesky.577), custom_call_target="Cholesky" | custom-call | tf_op jit(solution)/shard_map/jit(cholesky)/cholesky | solution.py:26
  492.3 9.8 %custom-call.64 = f32[1,128,128]{1,2,0:T(8,128)S(1)} custom-call(f32[1,128,128]{2,1,0:T(8,128)S(1)} %get-tuple-element.52), custom_call_target="InvertDiagBlocksLowerTriangular" | custom-call | tf_op jit(solution)/shard_map/jit(cholesky)/cholesky | solution.py:26
  505.3 11.7 %cholesky.243 = f32[128,128]{1,0:T(8,128)S(1)} custom-call(f32[128,128]{1,0:T(8,128)S(1)} %cholesky.581), custom_call_target="Cholesky" | custom-call | tf_op jit(solution)/shard_map/jit(cholesky)/cholesky | solution.py:26
  520.3 9.8 %custom-call.65 = f32[1,128,128]{1,2,0:T(8,128)S(1)} custom-call(f32[1,128,128]{2,1,0:T(8,128)S(1)} %get-tuple-element.50), custom_call_target="InvertDiagBlocksLowerTriangular" | custom-call | tf_op jit(solution)/shard_map/jit(cholesky)/cholesky | solution.py:26
  535.6 11.7 %cholesky.466 = f32[128,128]{1,0:T(8,128)S(1)} custom-call(f32[128,128]{1,0:T(8,128)S(1)} %cholesky.586), custom_call_target="Cholesky" | custom-call | tf_op jit(solution)/shard_map/jit(cholesky)/cholesky | solution.py:26
  548.1 9.8 %custom-call.66 = f32[1,128,128]{1,2,0:T(8,128)S(1)} custom-call(f32[1,128,128]{2,1,0:T(8,128)S(1)} %get-tuple-element.48), custom_call_target="InvertDiagBlocksLowerTriangular" | custom-call | tf_op jit(solution)/shard_map/jit(cholesky)/cholesky | solution.py:26
  562.5 11.7 %cholesky.485 = f32[128,128]{1,0:T(8,128)S(1)} custom-call(f32[128,128]{1,0:T(8,128)S(1)} %cholesky.591), custom_call_target="Cholesky" | custom-call | tf_op jit(solution)/shard_map/jit(cholesky)/cholesky | solution.py:26
  575.0 9.8 %custom-call.67 = f32[1,128,128]{1,2,0:T(8,128)S(1)} custom-call(f32[1,128,128]{2,1,0:T(8,128)S(1)} %get-tuple-element.46), custom_call_target="InvertDiagBlocksLowerTriangular" | custom-call | tf_op jit(solution)/shard_map/jit(cholesky)/cholesky | solution.py:26
  589.1 11.9 %cholesky.504 = f32[128,128]{1,0:T(8,128)S(1)} custom-call(f32[128,128]{1,0:T(8,128)S(1)} %cholesky.596), custom_call_target="Cholesky" | custom-call | tf_op jit(solution)/shard_map/jit(cholesky)/cholesky | solution.py:26
  601.8 9.8 %custom-call.68 = f32[1,128,128]{1,2,0:T(8,128)S(1)} custom-call(f32[1,128,128]{2,1,0:T(8,128)S(1)} %get-tuple-element.44), custom_call_target="InvertDiagBlocksLowerTriangular" | custom-call | tf_op jit(solution)/shard_map/jit(cholesky)/cholesky | solution.py:26
  615.8 11.7 %cholesky.524 = f32[128,128]{1,0:T(8,128)S(1)} custom-call(f32[128,128]{1,0:T(8,128)S(1)} %cholesky.601), custom_call_target="Cholesky" | custom-call | tf_op jit(solution)/shard_map/jit(cholesky)/cholesky | solution.py:26
  628.3 9.8 %custom-call.69 = f32[1,128,128]{1,2,0:T(8,128)S(1)} custom-call(f32[1,128,128]{2,1,0:T(8,128)S(1)} %get-tuple-element.42), custom_call_target="InvertDiagBlocksLowerTriangular" | custom-call | tf_op jit(solution)/shard_map/jit(cholesky)/cholesky | solution.py:26
  642.2 11.7 %cholesky.544 = f32[128,128]{1,0:T(8,128)S(1)} custom-call(f32[128,128]{1,0:T(8,128)S(1)} %cholesky.606), custom_call_target="Cholesky" | custom-call | tf_op jit(solution)/shard_map/jit(cholesky)/cholesky | solution.py:26
  654.7 9.8 %custom-call.70 = f32[1,128,128]{1,2,0:T(8,128)S(1)} custom-call(f32[1,128,128]{2,1,0:T(8,128)S(1)} %get-tuple-element.40), custom_call_target="InvertDiagBlocksLowerTriangular" | custom-call | tf_op jit(solution)/shard_map/jit(cholesky)/cholesky | solution.py:26
  667.5 11.7 %cholesky.562 = f32[128,128]{1,0:T(8,128)S(1)} custom-call(f32[128,128]{1,0:T(8,128)S(1)} %convolution_subtract_fusion.6), custom_call_target="Cholesky" | custom-call | tf_op jit(solution)/shard_map/jit(cholesky)/cholesky | solution.py:26
  689.4 4.9 select_select_fusion
  694.3 24.5 %while.1 = (s32[]{:T(128)}, f32[1024,1024]{0,1:T(8,128)}, s32[8,2]{0,1:T(2,128)S(1)}, f32[8,128,128]{2,1,0:T(8,128)S(1)}, s32[]{:T(128)}) while((s32[]{:T(128)}, f32[1024,1024]{0,1:T(8,128)}, s32[8,2]{0,1:T(2,128)S(1)}, f32[8,128,128]{2,1,0:T(8,128)S(1)}, s32[]{:T(128)}) %tuple.52), condition=%wide.while_cond, body=%wide.while_body.sunk | while | flops 2 | bytes 393321 | solution.py:28
  718.7 78.8 %custom-call.71 = f32[8,128,128]{1,2,0:T(8,128)S(1)} custom-call(f32[8,128,128]{2,1,0:T(8,128)S(1)} %get-tuple-element.12), custom_call_target="InvertDiagBlocksLowerTriangular" | custom-call | tf_op jit(solution)/shard_map/triangular_solve | solution.py:28
  818.5 5.7 fusion.125
  824.8 63.9 %psum.15 = f32[]{:T(128)} all-reduce(f32[]{:T(128)} %multiply_reduce_fusion), channel_id=1, replica_groups=mesh['smp'=32,'col'=2,'slab'=2] {'smp','col','slab'}, use_global_device_ids=true, to_apply=%region_21.22 | all-reduce | flops 1 | bytes 8 | tf_op jit(solution)/shard_map/psum | solution.py:32
  (171 shorter events, 107.1 us)
Async XLA Ops:
  6.5 453.8 %all-reduce.4.cloned.1.call-start = ((), (), s32[]{:S(2)}) async-start(), calls=%async_computation.1 | async-start | bytes 8388608 | tf_op jit(solution)/shard_map/psum | solution.py:24
  285.7 3.2 copy-start
  305.5 0.7 copy-start.3
  305.5 2.0 copy-start.2
  478.6 2.0 copy-start.1
Sparse Core Ops, SparseCore 0:
  305.7 154.5 all-reduce.3
where the time goes:
time: 904 us; the launch traced here: 897 us
  other arithmetic  279 us (31%)
  blocking collectives  235 us (26%)
  local copies, waits for them, and re-layouts  219 us (24%)
  waiting for transfers between devices  73 us (8%)
  matrix products  70 us (8%)
  between operations  21.6 us (2%)
    another operation x30, other arithmetic, shards(): jnp.linalg.cholesky(gram + shift * jnp.eye(samples, dtype=jnp.float32))  167 us
    unnamed x33, local copies, waits for them, and re-layouts  135 us
    all_to_all x1, blocking collectives, shards(): lax.all_to_all(jacobian, 'smp', split_axis=2, concat_axis=0, tiled=True)  105 us
    another operation x3, other arithmetic, shards(): lax.linalg.triangular_solve(factor, middle, left_side=True, lower=True, t...  83.6 us
    psum x1, waiting for transfers between devices, shards(): gram = lax.psum(partial_gram, ('smp', 'col', 'slab'))  73 us
    unnamed x1, blocking collectives  65.8 us
    psum x1, blocking collectives, shards(): squared = lax.psum(jnp.sum(delta * delta), ('smp', 'col', 'slab'))  63.9 us
    convert_element_type x1, local copies, waits for them, and re-layouts, shards(): values = columns.astype(jnp.float32)  44 us
  transfers between devices with their start and end apart: 1, of which 1 were waited for; matrix products, arithmetic and copies ran while one was open for 2% of the time, Pallas kernels for 0%

commit v1 on v0

--- a/solution.py
+++ b/solution.py
@@ -12,7 +12,10 @@
     samples = energies.shape[0]
     root_count = jnp.sqrt(jnp.float32(samples))
     eps = (energies - jnp.mean(energies)) / root_count
-    columns = lax.all_to_all(jacobian, "smp", split_axis=2, concat_axis=0, tiled=True)
+    columns = jnp.concatenate(
+        lax.all_to_all(jnp.stack(jnp.split(jacobian, lax.axis_size("smp"), axis=2)), "smp", 0, 0),
+        axis=0,
+    )
     slab_count = columns.shape[1]
     width = columns.shape[2]
     values = columns.astype(jnp.float32)

time: 904 us -> 782 us (0.87)
  local copies, waits for them, and re-layouts: 219 us -> 89.4 us
    unnamed x33 -> x61, local copies, waits for them, and re-layouts: 135 us -> 48.8 us
    convert_element_type x1 -> x0, local copies, waits for them, and re-layouts: 44 us -> none  [shards(): values = columns.astype(jnp.float32)]
    another operation x40 -> x41, local copies, waits for them, and re-layouts: 24.2 us -> 25.2 us
where the time goes in v1:
time: 782 us; the launch traced here: 770 us
  other arithmetic  275 us (35%)
  blocking collectives  234 us (30%)
  local copies, waits for them, and re-layouts  89.4 us (11%)
  matrix products  76.8 us (10%)
  waiting for transfers between devices  73.2 us (9%)
  between operations  21.6 us (3%)
    another operation x30, other arithmetic, shards(): jnp.linalg.cholesky(gram + shift * jnp.eye(samples, dtype=jnp.float32))  167 us
    all_to_all x1, blocking collectives, shards(): lax.all_to_all(jnp.stack(jnp.split(jacobian, lax.axis_size('smp'), axis=2...  104 us
    another operation x3, other arithmetic, shards(): lax.linalg.triangular_solve(factor, middle, left_side=True, lower=True, t...  83.6 us
    psum x1, waiting for transfers between devices, shards(): gram = lax.psum(partial_gram, ('smp', 'col', 'slab'))  73.1 us
    unnamed x1, blocking collectives  66 us
    psum x1, blocking collectives, shards(): squared = lax.psum(jnp.sum(delta * delta), ('smp', 'col', 'slab'))  63.9 us
    unnamed x61, local copies, waits for them, and re-layouts  48.8 us
    another operation x14, matrix products, shards(): jnp.linalg.cholesky(gram + shift * jnp.eye(samples, dtype=jnp.float32))  27.1 us
  transfers between devices with their start and end apart: 1, of which 1 were waited for; matrix products, arithmetic and copies ran while one was open for 2% of the time, Pallas kernels for 0%

profile of v1, /device:TPU:1, one launch (start us, length us, event | category | flops | bytes accessed | tf_op | source)
XLA Modules:
  0.0 769.9 jit_solution(2119023692501416147)
XLA Ops:
  37.7 104.2 %all_to_all.5 = bf16[32,32,16,256]{3,2,1,0:T(8,128)(2,1)S(1)} all-to-all(bf16[32,32,16,256]{3,2,1,0:T(8,128)(2,1)S(1)} %bitcast_dynamic-update-slice_fusion.1), channel_id=1, replica_groups=mesh['smp'=32,'col'=2,'slab'=2] {'smp'}, dimensions={0} | all-to-all | bytes 16777216 | tf_op jit(solution)/shard_map/all_to_all | solution.py:16
  141.9 3.2 copy-done
  146.3 8.9 %fusion.1 = bf16[32,32,16,256]{3,2,1,0:T(8,128)(2,1)} fusion(bf16[32,32,16,256]{3,2,1,0:T(8,128)(2,1)} %copy-done, f32[16,256]{1,0:T(8,128)S(1)} %broadcast_multiply_fusion.1), kind=kLoop, calls=%fused_computation.5 | loop fusion | flops 16777216 | bytes 16793600 | tf_op jit(solution)/shard_map/convert_element_type | solution.py:24
  155.2 23.4 %fusion.5 = f32[1024,1024]{0,1:T(8,128)} fusion(bf16[1024,16,256]{2,1,0:T(8,128)(2,1)} %bitcast.393), kind=kOutput, calls=%fused_computation.15 | convolution fusion | flops 8589934592 | bytes 12582912 | tf_op jit(solution)/shard_map/dot_general | solution.py:26
  180.4 66.0 %all-reduce.1 = f32[1024]{0:T(1024)S(1)} all-reduce(f32[1024]{0:T(1024)S(1)} %dynamic-update-slice.47), channel_id=1, replica_groups=mesh['smp'=32,'col'=2,'slab'=2] {'smp'}, use_global_device_ids=true, to_apply=%add.1 | all-reduce | flops 1024 | bytes 8192
  247.7 12.3 %copy.32 = bf16[128,8,16,256]{3,1,2,0:T(8,128)(2,1)} copy(bf16[128,8,16,256]{3,2,1,0:T(8,128)(2,1)} %bitcast.394) | data formatting | bytes 16777216
  260.0 73.1 %all-reduce.4.cloned.1.call-done = f32[1024,1024]{0,1:T(8,128)} async-done(((f32[1024,1024]{0,1:T(8,128)}), f32[1024,1024]{0,1:T(8,128)}) %all-reduce.4.cloned.1.call-update) | async-done | bytes 4194320 | tf_op jit(solution)/shard_map/psum | solution.py:27
  336.6 4.8 select_add_fusion
  341.4 5.5 copy.6
  347.0 4.5 fusion.4
  353.4 11.7 %cholesky.222 = f32[128,128]{1,0:T(8,128)S(1)} custom-call(f32[128,128]{1,0:T(8,128)S(1)} %cholesky.577), custom_call_target="Cholesky" | custom-call | tf_op jit(solution)/shard_map/jit(cholesky)/cholesky | solution.py:29
  365.3 9.8 %custom-call.64 = f32[1,128,128]{1,2,0:T(8,128)S(1)} custom-call(f32[1,128,128]{2,1,0:T(8,128)S(1)} %get-tuple-element.40), custom_call_target="InvertDiagBlocksLowerTriangular" | custom-call | tf_op jit(solution)/shard_map/jit(cholesky)/cholesky | solution.py:29
  378.4 11.7 %cholesky.243 = f32[128,128]{1,0:T(8,128)S(1)} custom-call(f32[128,128]{1,0:T(8,128)S(1)} %cholesky.581), custom_call_target="Cholesky" | custom-call | tf_op jit(solution)/shard_map/jit(cholesky)/cholesky | solution.py:29
  393.1 9.8 %custom-call.65 = f32[1,128,128]{1,2,0:T(8,128)S(1)} custom-call(f32[1,128,128]{2,1,0:T(8,128)S(1)} %get-tuple-element.38), custom_call_target="InvertDiagBlocksLowerTriangular" | custom-call | tf_op jit(solution)/shard_map/jit(cholesky)/cholesky | solution.py:29
  408.5 11.7 %cholesky.466 = f32[128,128]{1,0:T(8,128)S(1)} custom-call(f32[128,128]{1,0:T(8,128)S(1)} %cholesky.586), custom_call_target="Cholesky" | custom-call | tf_op jit(solution)/shard_map/jit(cholesky)/cholesky | solution.py:29
  421.0 9.8 %custom-call.66 = f32[1,128,128]{1,2,0:T(8,128)S(1)} custom-call(f32[1,128,128]{2,1,0:T(8,128)S(1)} %get-tuple-element.36), custom_call_target="InvertDiagBlocksLowerTriangular" | custom-call | tf_op jit(solution)/shard_map/jit(cholesky)/cholesky | solution.py:29
  432.0 3.3 convolution_subtract_fusion.2
  435.3 11.7 %cholesky.485 = f32[128,128]{1,0:T(8,128)S(1)} custom-call(f32[128,128]{1,0:T(8,128)S(1)} %cholesky.591), custom_call_target="Cholesky" | custom-call | tf_op jit(solution)/shard_map/jit(cholesky)/cholesky | solution.py:29
  447.8 9.8 %custom-call.67 = f32[1,128,128]{1,2,0:T(8,128)S(1)} custom-call(f32[1,128,128]{2,1,0:T(8,128)S(1)} %get-tuple-element.34), custom_call_target="InvertDiagBlocksLowerTriangular" | custom-call | tf_op jit(solution)/shard_map/jit(cholesky)/cholesky | solution.py:29
  458.7 3.2 convolution_subtract_fusion.3
  461.9 11.9 %cholesky.504 = f32[128,128]{1,0:T(8,128)S(1)} custom-call(f32[128,128]{1,0:T(8,128)S(1)} %cholesky.596), custom_call_target="Cholesky" | custom-call | tf_op jit(solution)/shard_map/jit(cholesky)/cholesky | solution.py:29
  474.6 9.8 %custom-call.68 = f32[1,128,128]{1,2,0:T(8,128)S(1)} custom-call(f32[1,128,128]{2,1,0:T(8,128)S(1)} %get-tuple-element.32), custom_call_target="InvertDiagBlocksLowerTriangular" | custom-call | tf_op jit(solution)/shard_map/jit(cholesky)/cholesky | solution.py:29
  488.6 11.7 %cholesky.524 = f32[128,128]{1,0:T(8,128)S(1)} custom-call(f32[128,128]{1,0:T(8,128)S(1)} %cholesky.601), custom_call_target="Cholesky" | custom-call | tf_op jit(solution)/shard_map/jit(cholesky)/cholesky | solution.py:29
  501.1 9.8 %custom-call.69 = f32[1,128,128]{1,2,0:T(8,128)S(1)} custom-call(f32[1,128,128]{2,1,0:T(8,128)S(1)} %get-tuple-element.30), custom_call_target="InvertDiagBlocksLowerTriangular" | custom-call | tf_op jit(solution)/shard_map/jit(cholesky)/cholesky | solution.py:29
  515.0 11.7 %cholesky.544 = f32[128,128]{1,0:T(8,128)S(1)} custom-call(f32[128,128]{1,0:T(8,128)S(1)} %cholesky.606), custom_call_target="Cholesky" | custom-call | tf_op jit(solution)/shard_map/jit(cholesky)/cholesky | solution.py:29
  527.5 9.8 %custom-call.70 = f32[1,128,128]{1,2,0:T(8,128)S(1)} custom-call(f32[1,128,128]{2,1,0:T(8,128)S(1)} %get-tuple-element.28), custom_call_target="InvertDiagBlocksLowerTriangular" | custom-call | tf_op jit(solution)/shard_map/jit(cholesky)/cholesky | solution.py:29
  540.3 11.7 %cholesky.562 = f32[128,128]{1,0:T(8,128)S(1)} custom-call(f32[128,128]{1,0:T(8,128)S(1)} %convolution_subtract_fusion.6), custom_call_target="Cholesky" | custom-call | tf_op jit(solution)/shard_map/jit(cholesky)/cholesky | solution.py:29
  562.2 4.9 select_select_fusion
  567.1 24.5 %while.1 = (s32[]{:T(128)}, f32[1024,1024]{0,1:T(8,128)}, s32[8,2]{0,1:T(2,128)S(1)}, f32[8,128,128]{2,1,0:T(8,128)S(1)}, s32[]{:T(128)}) while((s32[]{:T(128)}, f32[1024,1024]{0,1:T(8,128)}, s32[8,2]{0,1:T(2,128)S(1)}, f32[8,128,128]{2,1,0:T(8,128)S(1)}, s32[]{:T(128)}) %tuple.49), condition=%wide.while_cond, body=%wide.while_body.sunk | while | flops 2 | bytes 393329 | solution.py:31
  591.6 78.8 %custom-call.71 = f32[8,128,128]{1,2,0:T(8,128)S(1)} custom-call(f32[8,128,128]{2,1,0:T(8,128)S(1)} %get-tuple-element.12), custom_call_target="InvertDiagBlocksLowerTriangular" | custom-call | tf_op jit(solution)/shard_map/triangular_solve | solution.py:31
  691.3 5.7 fusion.125
  697.6 63.9 %psum.15 = f32[]{:T(128)} all-reduce(f32[]{:T(128)} %multiply_reduce_fusion), channel_id=1, replica_groups=mesh['smp'=32,'col'=2,'slab'=2] {'smp','col','slab'}, use_global_device_ids=true, to_apply=%region_21.22 | all-reduce | flops 1 | bytes 8 | tf_op jit(solution)/shard_map/psum | solution.py:35
  (199 shorter events, 119.9 us)
Async XLA Ops:
  6.5 326.6 %all-reduce.4.cloned.1.call-start = ((), (), s32[]{:S(2)}) async-start(), calls=%async_computation.1 | async-start | bytes 8388608 | tf_op jit(solution)/shard_map/psum | solution.py:27
  141.9 3.2 copy-start
  155.2 23.5 %copy-start.3 = (u32[128]{0:T(128)S(1)}, u32[128]{0:T(128)}, u32[]{:S(2)}) copy-start(u32[128]{0:T(128)} %constant.323) | copy-start | bytes 1540
  155.2 24.7 %copy-start.2 = (f32[32]{0:T(128)S(1)}, f32[32]{0:T(128)}, u32[]{:S(2)}) copy-start(f32[32]{0:T(128)} %param.3) | copy-start | bytes 388
  351.4 2.0 copy-start.1
Sparse Core Ops, SparseCore 0:
  178.8 154.3 all-reduce.3
